TPU v7x, 256 devices: a whole 4x4x8 slice. The times are simulated.
256 devices in a mesh: lat: 16 (over y_lo, x, core), lon: 16 (over z, y_hi).
Axes of the slice: x: 4, y: 4 (y_hi: 2, y_lo: 2; y = y_hi * 2 + y_lo), z: 8, core: 2. Of those that a mesh axis runs over, the one named last changes fastest.
Arguments:
- fields: bfloat16 [512, 512, 256], P('lat', 'lon'), may hold values from -6 to 6
- w_conv1: bfloat16 [3, 3, 256, 256], replicated, may hold values from -0.125 to 0.125
- b_conv1: float32 [256], replicated, may hold values from -3 to 3
- w_conv2: bfloat16 [3, 3, 256, 256], replicated, may hold values from -0.125 to 0.125
- b_conv2: float32 [256], replicated, may hold values from -3 to 3
- w_query: bfloat16 [256, 256], replicated, may hold values from -16 to 16
- w_key: bfloat16 [256, 64], replicated, may hold values from -1 to 1
- w_value: bfloat16 [256, 64], replicated, may hold values from -0.375 to 0.375
- w_out: bfloat16 [256, 256], replicated, may hold values from -0.375 to 0.375
- rotation: int32 [16, 16], replicated, may hold values from 0 to 3
- owner: int32 [16, 16], replicated, may hold values from 0 to 15, as said below
- counts: int32 [512], replicated, may hold values from 4 to 512
Outputs:
- fields_out: bfloat16 [512, 512, 256], P('lat', 'lon')
Inputs may be any that keep to these rules, and one draw needn't show every extreme that they name: Each row of owner holds every number from 0 to 15 exactly once.
All inputs are finite; a program needn't handle non-finite values.
Results may differ from a plain program's by a relative error of at most 0.014.
Values may be sent and summed in bfloat16 or wider, within the bound.
A program may use at most 64 MiB of HBM per device.

v0:
```python
import math

import jax
import jax.numpy as jnp
from jax import lax
from jax.sharding import PartitionSpec as P


def shortened(x):

    def short(part):
        return part.astype(jnp.bfloat16) if part.dtype == jnp.float32 else part

    return jax.tree.map(short, x)


def passed_along(x, axis, by):
    devices = lax.axis_size(axis)
    pairs = [(i, i + by) for i in range(devices) if 0 <= i + by < devices]
    return lax.ppermute(x, axis, pairs)


def turn_block(block, quarter_turns):
    options = [lambda m, k=k: jnp.rot90(m, k, axes=(0, 1)) for k in range(4)]
    return lax.switch(quarter_turns % 4, options, block)


def inverse_owner(owner):
    shards = jnp.arange(owner.shape[1], dtype=jnp.int32)
    matches = owner[:, None, :] == shards[None, :, None]
    return jnp.sum(jnp.where(matches, shards[None, None, :], 0), axis=2)


def live_region(counts, first_row, row_count, first_col, col_count, total_cols):
    padded_counts = jnp.pad(counts, 2)
    row_limits = lax.dynamic_slice_in_dim(padded_counts, first_row + 2, row_count)
    columns = (first_col + jnp.arange(col_count, dtype=jnp.int32)) % total_cols
    return (columns[None, :] < row_limits[:, None]).astype(jnp.float32)


def pick_block(stack, inverse, band_row, segment):
    return lax.dynamic_index_in_dim(stack, inverse[band_row, segment], 0, keepdims=False)


def fetch_halo(part, width, inverse, band_index, segment):
    lat_size = lax.axis_size("lat")
    lon_size = lax.axis_size("lon")
    block_size = part.shape[0]
    chans = part.shape[2]
    from_north = passed_along(shortened(part[-width:]), "lat", 1)
    from_south = passed_along(shortened(part[:width]), "lat", -1)
    west_all, east_all, north_all, south_all = (
        lax.all_gather(shortened(part[:, :width]), "lon", axis=0, tiled=True),
        lax.all_gather(shortened(part[:, -width:]), "lon", axis=0, tiled=True),
        lax.all_gather(shortened(from_north), "lon", axis=0, tiled=True).astype(from_north.dtype),
        lax.all_gather(shortened(from_south), "lon", axis=0, tiled=True).astype(from_south.dtype),
    )
    west_all = west_all.reshape(lon_size, block_size, width, chans)
    east_all = east_all.reshape(lon_size, block_size, width, chans)
    north_all = north_all.reshape(lon_size, width, block_size, chans)
    south_all = south_all.reshape(lon_size, width, block_size, chans)
    west_segment = (segment - 1) % lon_size
    east_segment = (segment + 1) % lon_size
    north_band = jnp.maximum(band_index - 1, 0)
    south_band = jnp.minimum(band_index + 1, lat_size - 1)
    left_cols = pick_block(east_all, inverse, band_index, west_segment)
    right_cols = pick_block(west_all, inverse, band_index, east_segment)
    upper = jnp.concatenate(
        [
            pick_block(north_all, inverse, north_band, west_segment)[:, -width:],
            pick_block(north_all, inverse, north_band, segment),
            pick_block(north_all, inverse, north_band, east_segment)[:, :width],
        ],
        axis=1,
    )
    lower = jnp.concatenate(
        [
            pick_block(south_all, inverse, south_band, west_segment)[:, -width:],
            pick_block(south_all, inverse, south_band, segment),
            pick_block(south_all, inverse, south_band, east_segment)[:, :width],
        ],
        axis=1,
    )
    middle = jnp.concatenate([left_cols, part, right_cols], axis=1)
    return jnp.concatenate([upper, middle, lower], axis=0)


def convolve(padded, weight, bias, out_rows, out_cols):
    chans = padded.shape[2]
    total = jnp.zeros((out_rows * out_cols, chans), jnp.float32) + bias
    for i in range(3):
        for j in range(3):
            window = padded[i : i + out_rows, j : j + out_cols].reshape(out_rows * out_cols, chans)
            total = total + jnp.dot(window, weight[i, j], preferred_element_type=jnp.float32)
    return total.reshape(out_rows, out_cols, chans)


def on_device(
    fields,
    w_conv1,
    b_conv1,
    w_conv2,
    b_conv2,
    w_query,
    w_key,
    w_value,
    w_out,
    rotation,
    owner,
    counts,
):
    block_size = fields.shape[0]
    chans = fields.shape[2]
    head_dim = w_key.shape[1]
    heads = chans // head_dim
    lon_size = lax.axis_size("lon")
    band_index = lax.axis_index("lat")
    shard_index = lax.axis_index("lon")
    quarter = rotation[band_index, shard_index]
    segment = owner[band_index, shard_index]
    owner_row = owner[band_index]
    inverse = inverse_owner(owner)
    upright = turn_block(fields, (4 - quarter) % 4)
    total_cols = block_size * lon_size
    first_row = band_index * block_size
    first_col = segment * block_size
    live_own = live_region(counts, first_row, block_size, first_col, block_size, total_cols)[
        :, :, None
    ]
    padded = fetch_halo(upright, 1, inverse, band_index, segment)
    first = convolve(padded, w_conv1, b_conv1, block_size, block_size)
    act = (jax.nn.silu(first) * live_own).astype(jnp.bfloat16)
    act_padded = fetch_halo(act, 1, inverse, band_index, segment)
    second = convolve(act_padded, w_conv2, b_conv2, block_size, block_size)
    mixed = ((upright.astype(jnp.float32) + second) * live_own).astype(jnp.bfloat16)
    flat = mixed.reshape(block_size * block_size, chans).astype(jnp.float32)
    normed = (flat * lax.rsqrt(jnp.mean(flat * flat, axis=1, keepdims=True) + 1e-06)).astype(
        jnp.bfloat16
    )
    query = jnp.dot(normed, w_query, preferred_element_type=jnp.float32).astype(jnp.bfloat16)
    query = query.reshape(block_size, block_size, chans)
    key_val = jnp.dot(
        normed, jnp.concatenate([w_key, w_value], axis=1), preferred_element_type=jnp.float32
    )
    key_val = key_val.astype(jnp.bfloat16).reshape(block_size, block_size, 2 * head_dim)
    root_dim = math.sqrt(head_dim)
    heads_q = query.reshape(block_size, block_size, heads, head_dim)
    row_limits = lax.dynamic_slice_in_dim(counts, first_row, block_size)
    piece = lax.all_gather(key_val, "lon", axis=1, tiled=True)
    summed = jnp.zeros((block_size, block_size, heads, head_dim), jnp.float32)
    peak = jnp.full((block_size, block_size, heads), -jnp.inf, jnp.float32)
    total = jnp.zeros((block_size, block_size, heads), jnp.float32)
    positions = jnp.arange(piece.shape[1], dtype=jnp.int32)
    true_cols = owner_row[positions // block_size] * block_size + positions % block_size
    live_keys = true_cols[None, :] < row_limits[:, None]
    scores = (
        jnp.einsum(
            "rchd,rkd->rchk", heads_q, piece[:, :, :head_dim], preferred_element_type=jnp.float32
        )
        / root_dim
    )
    scores = jnp.where(live_keys[:, None, None, :], scores, -jnp.inf)
    new_peak = jnp.max(scores, axis=3)
    safe_peak = jnp.where(jnp.isfinite(new_peak), new_peak, 0.0)
    expo = jnp.exp(scores - safe_peak[..., None])
    shrink = jnp.exp(peak - safe_peak)
    total = total * shrink + jnp.sum(expo, axis=3)
    summed = summed * shrink[..., None] + jnp.einsum(
        "rchk,rkd->rchd",
        expo.astype(jnp.bfloat16),
        piece[:, :, head_dim:],
        preferred_element_type=jnp.float32,
    )
    summed, peak, total = (summed, new_peak, total)
    attended = (
        (summed / total[..., None]).astype(jnp.bfloat16).reshape(block_size * block_size, chans)
    )
    update = jnp.dot(attended, w_out, preferred_element_type=jnp.float32).reshape(
        block_size, block_size, chans
    )
    result = (mixed.astype(jnp.float32) + update * live_own).astype(jnp.bfloat16)
    return turn_block(result, quarter)


def solution(mesh):
    in_specs = (P("lat", "lon", None), P(), P(), P(), P(), P(), P(), P(), P(), P(), P(), P())
    out_specs = P("lat", "lon", None)
    return jax.shard_map(
        on_device, mesh=mesh, in_specs=in_specs, out_specs=out_specs, check_vma=False
    )
```

profile of v0, /device:TPU:2, one launch (start us, length us, event | category | flops | bytes accessed | tf_op | source)
XLA Modules:
  0.0 502.5 jit_solution(5571521871443634493)
XLA Ops:
  8.5 1.4 conditional.2
  8.5 1.3 copy.100
  10.2 1.9 collective-permute-start.1
  12.1 2.4 collective-permute-start
  23.2 45.6 %all_gather.28 = bf16[512,1,256]{2,0,1:T(8,128)(2,1)S(1)} all-gather(bf16[32,1,256]{2,0,1:T(8,128)(2,1)S(1)} %get-tuple-element.55), channel_id=1, replica_groups=mesh['lat'=16,'lon'=16] {'lon'}, dimensions={0}, use_global_device_ids=true | all-gather | bytes 278528 | tf_op jit(solution)/shard_map/all_gather | solution.py:54
  69.4 36.9 %all_gather.29 = bf16[512,1,256]{2,0,1:T(8,128)(2,1)S(1)} all-gather(bf16[32,1,256]{2,0,1:T(8,128)(2,1)S(1)} %get-tuple-element.56), channel_id=1, replica_groups=mesh['lat'=16,'lon'=16] {'lon'}, dimensions={0}, use_global_device_ids=true | all-gather | bytes 278528 | tf_op jit(solution)/shard_map/all_gather | solution.py:53
  118.9 40.5 %all_gather.27 = bf16[16,32,256]{2,1,0:T(8,128)(2,1)S(1)} all-gather(bf16[1,32,256]{2,1,0:T(8,128)(2,1)S(1)} %collective-permute-done), channel_id=1, replica_groups=mesh['lat'=16,'lon'=16] {'lon'}, dimensions={0}, use_global_device_ids=true | all-gather | bytes 278528 | tf_op jit(solution)/shard_map/all_gather | solution.py:55
  159.5 37.0 %all_gather.30 = bf16[16,32,256]{2,1,0:T(8,128)(2,1)S(1)} all-gather(bf16[1,32,256]{2,1,0:T(8,128)(2,1)S(1)} %collective-permute-done.1), channel_id=1, replica_groups=mesh['lat'=16,'lon'=16] {'lon'}, dimensions={0}, use_global_device_ids=true | all-gather | bytes 278528 | tf_op jit(solution)/shard_map/all_gather | solution.py:56
  201.4 1.9 collective-permute-start.3
  203.3 2.4 collective-permute-start.2
  205.8 40.4 %all_gather.33 = bf16[512,1,256]{2,0,1:T(8,128)(2,1)S(1)} all-gather(bf16[32,1,256]{2,0,1:T(8,128)(2,1)S(1)} %copy.114), channel_id=1, replica_groups=mesh['lat'=16,'lon'=16] {'lon'}, dimensions={0}, use_global_device_ids=true | all-gather | bytes 278528 | tf_op jit(solution)/shard_map/all_gather | solution.py:53
  246.2 37.0 %all_gather.32 = bf16[512,1,256]{2,0,1:T(8,128)(2,1)S(1)} all-gather(bf16[32,1,256]{2,0,1:T(8,128)(2,1)S(1)} %copy.113), channel_id=1, replica_groups=mesh['lat'=16,'lon'=16] {'lon'}, dimensions={0}, use_global_device_ids=true | all-gather | bytes 278528 | tf_op jit(solution)/shard_map/all_gather | solution.py:54
  283.7 40.4 %all_gather.31 = bf16[16,32,256]{2,1,0:T(8,128)(2,1)S(1)} all-gather(bf16[1,32,256]{2,1,0:T(8,128)(2,1)S(1)} %collective-permute-done.2), channel_id=1, replica_groups=mesh['lat'=16,'lon'=16] {'lon'}, dimensions={0}, use_global_device_ids=true | all-gather | bytes 278528 | tf_op jit(solution)/shard_map/all_gather | solution.py:55
  324.2 37.2 %all_gather.34 = bf16[16,32,256]{2,1,0:T(8,128)(2,1)S(1)} all-gather(bf16[1,32,256]{2,1,0:T(8,128)(2,1)S(1)} %collective-permute-done.3), channel_id=1, replica_groups=mesh['lat'=16,'lon'=16] {'lon'}, dimensions={0}, use_global_device_ids=true | all-gather | bytes 278528 | tf_op jit(solution)/shard_map/all_gather | solution.py:56
  371.7 4.4 compare_select_fusion.1
  376.1 5.6 %fusion.63 = s32[512]{0:T(512)S(1)} fusion(pred[512]{0:T(512)(128)(4,1)S(1)} %get-tuple-element.95, pred[512]{0:T(512)(128)(4,1)S(1)} %get-tuple-element.96, pred[512]{0:T(512)(128)(4,1)S(1)} %get-tuple-element.97, pred[512]{0:T(512)(128)(4,1)S(1)} %get-tuple-element.98, pred[512]{0:T(512)(128)(4,1)S(1)} %get-tuple-element.99, ...), kind=kLoop, calls=%fused_computation.145 | loop fusion | flops 8704 | bytes 8740 | tf_op jit(solution)/shard_map/add | solution.py:154
  382.1 1.5 reshape_reshape.3
  383.6 83.3 %all-gather.2.cloned.1.call-done = bf16[32,512,128]{2,0,1:T(8,128)(2,1)} async-done(((bf16[32,32,128]{2,0,1:T(8,128)(2,1)}), bf16[32,512,128]{2,0,1:T(8,128)(2,1)}) %all-gather.2.cloned.1.call-update) | async-done | bytes 4194320 | tf_op jit(solution)/shard_map/all_gather | solution.py:149
  466.9 7.6 %fusion.74 = (bf16[32,512,64]{2,0,1:T(8,128)(2,1)}, bf16[32,512,64]{2,0,1:T(8,128)(2,1)}) fusion(bf16[32,512,128]{2,0,1:T(8,128)(2,1)} %all-gather.2.cloned.1.call-done), kind=kLoop, calls=%fused_computation.158 | loop fusion | bytes 8388608 | tf_op jit(solution)/shard_map/slice | solution.py:158
  474.5 4.5 copy.133
  479.0 5.5 %copy.134 = bf16[32,512,64]{1,2,0:T(8,128)(2,1)} copy(bf16[32,512,64]{2,0,1:T(8,128)(2,1)} %get-tuple-element.28) | data formatting | bytes 4194304
  484.4 2.5 fusion
  487.0 2.4 fusion.1
  489.5 2.9 divide_convert_fusion
  (113 shorter events, 21.4 us)
Async XLA Ops:
  6.5 375.3 %copy-start = (bf16[256,256]{1,0:T(8,128)(2,1)S(1)}, bf16[256,256]{1,0:T(8,128)(2,1)}, u32[]{:S(2)}) copy-start(bf16[256,256]{1,0:T(8,128)(2,1)} %param.25) | copy-start | bytes 393220
  6.5 460.4 %all-gather.2.cloned.1.call-start = ((), (), s32[]{:S(2)}) async-start(), calls=%async_computation | async-start | bytes 4456448 | tf_op jit(solution)/shard_map/all_gather | solution.py:149
  8.5 6.1 %copy-start.9 = (s32[16,16]{1,0:T(8,128)S(1)}, s32[16,16]{1,0:T(8,128)}, u32[]{:S(2)}) copy-start(s32[16,16]{1,0:T(8,128)} %param.30) | copy-start | bytes 3076
  8.5 14.3 %copy-start.10 = (s32[512]{0:T(512)S(1)}, s32[512]{0:T(512)}, u32[]{:S(2)}) copy-start(s32[512]{0:T(512)} %param.31) | copy-start | bytes 6148
  10.2 149.3 %collective-permute-start.1 = (bf16[1,32,256]{2,1,0:T(8,128)(2,1)S(1)}, bf16[1,32,256]{2,1,0:T(8,128)(2,1)S(1)}, u32[]{:S(2)}, u32[]{:S(2)}) collective-permute-start(bf16[1,32,256]{2,1,0:T(8,128)(2,1)S(1)} %get-tuple-element.51), channel_id=1, source_target_pairs={{16,0},{32,16},{48,32},{64,48},{80,64},{96,80},{112,96},{128,112},... | collective-permute-start | bytes 49160 | tf_op jit(solution)/shard_map/ppermute | solution.py:20
  12.1 106.8 %collective-permute-start = (bf16[1,32,256]{2,1,0:T(8,128)(2,1)S(1)}, bf16[1,32,256]{2,1,0:T(8,128)(2,1)S(1)}, u32[]{:S(2)}, u32[]{:S(2)}) collective-permute-start(bf16[1,32,256]{2,1,0:T(8,128)(2,1)S(1)} %get-tuple-element.52), channel_id=1, source_target_pairs={{0,16},{16,32},{32,48},{48,64},{64,80},{80,96},{96,112},{112,128},... | collective-permute-start | bytes 49160 | tf_op jit(solution)/shard_map/ppermute | solution.py:20
  197.0 1.3 copy-start.4
  197.0 1.3 copy-start.11
  201.4 122.8 %collective-permute-start.3 = (bf16[1,32,256]{2,1,0:T(8,128)(2,1)S(1)}, bf16[1,32,256]{2,1,0:T(8,128)(2,1)S(1)}, u32[]{:S(2)}, u32[]{:S(2)}) collective-permute-start(bf16[1,32,256]{2,1,0:T(8,128)(2,1)S(1)} %get-tuple-element.45), channel_id=1, source_target_pairs={{16,0},{32,16},{48,32},{64,48},{80,64},{96,80},{112,96},{128,112},... | collective-permute-start | bytes 49160 | tf_op jit(solution)/shard_map/ppermute | solution.py:20
  203.3 80.4 %collective-permute-start.2 = (bf16[1,32,256]{2,1,0:T(8,128)(2,1)S(1)}, bf16[1,32,256]{2,1,0:T(8,128)(2,1)S(1)}, u32[]{:S(2)}, u32[]{:S(2)}) collective-permute-start(bf16[1,32,256]{2,1,0:T(8,128)(2,1)S(1)} %get-tuple-element.46), channel_id=1, source_target_pairs={{0,16},{16,32},{32,48},{48,64},{64,80},{80,96},{96,112},{112,128},... | collective-permute-start | bytes 49160 | tf_op jit(solution)/shard_map/ppermute | solution.py:20
  362.3 1.3 copy-start.5
  362.3 1.3 copy-start.12
  367.0 0.8 copy-start.7
  367.0 0.8 copy-start.8
  487.0 2.5 copy-start.3
  492.4 1.2 copy-start.6
  494.0 0.8 copy-start.2
  494.8 0.9 copy-start.1
Sparse Core Ops, SparseCore 0:
  369.1 97.8 all-gather.1
where the time goes:
time: 504 us; the launch traced here: 503 us
  blocking collectives  315 us (62%)
  waiting for transfers between devices  83.4 us (17%)
  between operations  35.8 us (7%)
  local copies, waits for them, and re-layouts  31.6 us (6%)
  other arithmetic  16.2 us (3%)
  matrix products  11.8 us (2%)
  starting transfers between devices  8.66 us (2%)
    all_gather x1, waiting for transfers between devices, on_device(): piece = lax.all_gather(key_val, 'lon', axis=1, tiled=True)  83.3 us
    all_gather x2, blocking collectives, fetch_halo(): lax.all_gather(shortened(part[:, -width:]), 'lon', axis=0, tiled=True)  82.6 us
    all_gather x2, blocking collectives, fetch_halo(): lax.all_gather(shortened(from_north), 'lon', axis=0, tiled=True)  81 us
    all_gather x2, blocking collectives, fetch_halo(): lax.all_gather(shortened(part[:, :width]), 'lon', axis=0, tiled=True)  77.3 us
    all_gather x2, blocking collectives, fetch_halo(): lax.all_gather(shortened(from_south), 'lon', axis=0, tiled=True)  74.2 us
    unnamed x28, local copies, waits for them, and re-layouts  13.4 us
  transfers between devices with their start and end apart: 5, of which 1 were waited for; matrix products, arithmetic and copies ran while one was open for 3% of the time, Pallas kernels for 0%

commit v1 on v0

v1 whole, which is shorter than its diff:
```python
import functools
import math

import jax
import jax.numpy as jnp
from jax import lax
from jax.experimental import pallas as pl
from jax.experimental.pallas import tpu as pltpu
from jax.sharding import PartitionSpec as P

MESH = pl.DeviceIdType.MESH
C = 256
HEADS = 4
HEAD_DIM = 64
SIDE = 32
COLS = 512
SEGS = 16
GROUPS = 256
PIECE = 2 * SIDE
BF16 = jnp.bfloat16
F32 = jnp.float32


def row_group(lat, lon):
    pair, core = lat // 2, lat % 2
    z, high = lon // 2, lon % 2
    place = z + high * (15 - 2 * z)
    place = place + (pair % 2) * (15 - 2 * place)
    return 32 * pair + 2 * place + core


def holder(group):
    pair, rest = group // 32, group % 32
    place, core = rest // 2, rest % 2
    place = place + (pair % 2) * (15 - 2 * place)
    high = place // 8
    z = place + high * (15 - 2 * place)
    return 2 * pair + core, 2 * z + high


def turned(block, base, step_i, step_j, first, count):
    cells = lax.broadcasted_iota(jnp.int32, (count, 1), 0) + first
    source = base + step_i * (cells // SIDE) + step_j * (cells % SIDE)
    spots = lax.broadcasted_iota(jnp.int32, (count, SIDE * SIDE), 1)
    pick = jnp.where(spots == source, 1.0, 0.0).astype(BF16)
    return jnp.dot(pick, block, preferred_element_type=F32).astype(BF16)


def steps_of(quarter, upright):
    n = SIDE
    odd_a = (n * (n - 1), 1, -n)
    odd_b = (n - 1, -1, n)
    one, three = (odd_a, odd_b) if upright else (odd_b, odd_a)
    table = [(0, n, 1), one, (n * n - 1, -n, -1), three]

    def chosen(at):
        value = table[0][at]
        for k in (1, 2, 3):
            value = jnp.where(quarter == k, table[k][at], value)
        return value

    return chosen(0), chosen(1), chosen(2)


def section(
    rotation_ref, inverse_ref, owner_ref, counts_ref,
    fields_ref, w1_hbm, b1_ref, w2_hbm, b2_ref,
    wq_ref, wk_ref, wv_ref, wo_ref,
    out_ref,
    upright, raw_up, raw, raw_down, rows, acts, result, outgoing, w1, w2, wkv,
    send_in, recv_in, send_halo, recv_halo, send_out, recv_out, local_sem, weight_sem,
):
    lat, lon = lax.axis_index("lat"), lax.axis_index("lon")
    group = row_group(lat, lon)
    band = group // 16
    mine = band == lat
    barrier = pltpu.get_barrier_semaphore()

    def greet(device):
        @pl.when(jnp.logical_or(device[0] != lat, device[1] != lon))
        def _():
            pl.semaphore_signal(barrier, inc=1, device_id=device, device_id_type=MESH)

    def greet_all(j, carry):
        greet(holder(16 * lat + j))
        greet((band, j))
        return carry

    lax.fori_loop(0, 16, greet_all, 0)

    @pl.when(group > 0)
    def _():
        pl.semaphore_signal(barrier, inc=1, device_id=holder(group - 1), device_id_type=MESH)

    @pl.when(group < GROUPS - 1)
    def _():
        pl.semaphore_signal(barrier, inc=1, device_id=holder(group + 1), device_id_type=MESH)

    def weight_copies():
        for which, (source, target) in enumerate(((w1_hbm, w1), (w2_hbm, w2))):
            for i in range(3):
                for j in range(3):
                    yield pltpu.make_async_copy(
                        source.at[i, j],
                        target.at[pl.ds(C * i, C), pl.ds(C * j, C)],
                        weight_sem.at[which, 3 * i + j],
                    )

    for copy in weight_copies():
        copy.start()

    quarter = rotation_ref[lat, lon]
    base, step_i, step_j = steps_of(quarter, True)

    def turn(at, carry):
        part = turned(fields_ref[...], base, step_i, step_j, at * 256, 256)
        upright[pl.ds(4 * at, 4)] = part.reshape(4, PIECE, C)
        return carry

    lax.fori_loop(0, 4, turn, 0)

    @pl.when(group == 0)
    def _():
        raw_up[...] = jnp.zeros((SEGS, PIECE, C), BF16)

    @pl.when(group == GROUPS - 1)
    def _():
        raw_down[...] = jnp.zeros((SEGS, PIECE, C), BF16)

    key_part = wk_ref[...]
    value_part = wv_ref[...]
    blank = jnp.zeros((C, HEAD_DIM), BF16)
    wkv[...] = jnp.concatenate(
        [key_part, blank, blank, key_part, value_part, blank, blank, value_part], axis=1
    )

    own = jnp.where(mine, 1, 0)
    pl.semaphore_wait(
        barrier,
        2 * (16 - own) + jnp.where(group > 0, 1, 0) + jnp.where(group < GROUPS - 1, 1, 0),
    )

    def piece_copy(j):
        return pltpu.make_async_remote_copy(
            src_ref=upright.at[j],
            dst_ref=raw.at[lon],
            send_sem=send_in.at[j],
            recv_sem=recv_in.at[lon],
            device_id=holder(16 * lat + j),
            device_id_type=MESH,
        )

    def own_copy():
        return pltpu.make_async_copy(upright.at[group % 16], raw.at[lon], local_sem.at[0])

    @pl.when(mine)
    def _():
        own_copy().start()

    def send_piece(t, carry):
        j = (group + 1 + t) % 16

        @pl.when(16 * lat + j != group)
        def _():
            piece_copy(j).start()

        return carry

    lax.fori_loop(0, 16, send_piece, 0)

    def halo_copy(s, up):
        slot = 2 if up else 0
        return pltpu.make_async_remote_copy(
            src_ref=raw.at[s],
            dst_ref=(raw_down if up else raw_up).at[s],
            send_sem=send_halo.at[slot, s],
            recv_sem=recv_halo.at[slot, s],
            device_id=holder(group - 1 if up else group + 1),
            device_id_type=MESH,
        )

    def arrived(s):
        return pltpu.make_async_remote_copy(
            src_ref=upright.at[0],
            dst_ref=raw.at[s],
            send_sem=send_in.at[0],
            recv_sem=recv_in.at[s],
            device_id=(band, s),
            device_id_type=MESH,
        )

    def forward(t, carry):
        s = (lon + t) % 16
        here = jnp.logical_and(mine, s == lon)

        @pl.when(here)
        def _():
            own_copy().wait()

        @pl.when(jnp.logical_not(here))
        def _():
            arrived(s).wait_recv()

        @pl.when(group > 0)
        def _():
            halo_copy(s, True).start()

        @pl.when(group < GROUPS - 1)
        def _():
            halo_copy(s, False).start()

        return carry

    lax.fori_loop(0, 16, forward, 0)

    def place(slot):
        from_band = jnp.clip(group - 1 + slot, 0, GROUPS - 1) // 16
        for t in range(SEGS):
            s = inverse_ref[from_band, t]
            piece = (raw_up, raw, raw_down)[slot][s]
            for r in range(2):
                rows[pl.ds(SIDE * t, SIDE), pl.ds(C * (2 * slot + r), C)] = piece[
                    SIDE * r : SIDE * (r + 1)
                ]

    place(1)
    for copy in weight_copies():
        copy.wait()

    def wait_halo(s, carry):
        @pl.when(group < GROUPS - 1)
        def _():
            halo_copy(s, True).wait_recv()

        @pl.when(group > 0)
        def _():
            halo_copy(s, False).wait_recv()

        return carry

    lax.fori_loop(0, 16, wait_halo, 0)
    place(0)
    place(2)

    columns = lax.broadcasted_iota(jnp.int32, (COLS, 1), 0)

    def live_of(offset):
        row = 2 * group + offset
        inside = jnp.logical_and(row >= 0, row < 2 * GROUPS)
        count = jnp.where(inside, counts_ref[jnp.clip(row, 0, 2 * GROUPS - 1)], 0)
        return jnp.where(columns < count, 1.0, 0.0)

    def convolved(source, r, weight, bias_ref):
        taps = jnp.dot(
            source[:, C * r : C * (r + 3)], weight[...], preferred_element_type=F32
        )
        return (
            pltpu.roll(taps[:, :C], 1, 0)
            + taps[:, C : 2 * C]
            + pltpu.roll(taps[:, 2 * C :], COLS - 1, 0)
            + bias_ref[...]
        )

    def make_act(r):
        first = convolved(rows, r, w1, b1_ref)
        value = first / (1.0 + jnp.exp(-first))
        acts[:, C * r : C * (r + 1)] = (value * live_of(r - 1)).astype(BF16)

    scale = math.log2(math.e) / math.sqrt(HEAD_DIM)
    lanes = lax.broadcasted_iota(jnp.int32, (1, 2 * HEAD_DIM), 1)
    low = lanes < HEAD_DIM

    def make_row(r):
        live = live_of(r)
        second = convolved(acts, r, w2, b2_ref)
        grid = rows[:, C * (r + 2) : C * (r + 3)].astype(F32)
        mixed = ((grid + second) * live).astype(BF16)
        flat = mixed.astype(F32)
        mean = jnp.mean(flat * flat, axis=1, keepdims=True)
        normed = (flat * lax.rsqrt(mean + 1e-06)).astype(BF16)
        query = jnp.dot(normed, wq_ref[...], preferred_element_type=F32)
        key_val = jnp.dot(normed, wkv[...], preferred_element_type=F32)
        bias = jnp.where(live > 0, 0.0, -1e30)
        ones = jnp.broadcast_to(live, (COLS, 2 * HEAD_DIM)).astype(BF16)
        keys, values, marks = [], [], []
        for odd in range(2):
            spot = jnp.where(lanes == (0 if odd else HEAD_DIM), 1.0, 0.0)
            pair = key_val[:, 128 * odd : 128 * (odd + 1)]
            keys.append((pair + bias * spot).astype(BF16))
            pair = key_val[:, 256 + 128 * odd : 256 + 128 * (odd + 1)].astype(BF16)
            values.append(jnp.concatenate([pair, ones], axis=1))
            marks.append(spot)
        parts = []
        for h in range(HEADS):
            odd = h % 2
            pair = query[:, 128 * (h // 2) : 128 * (h // 2 + 1)]
            keep = jnp.logical_not(low) if odd else low
            head = jnp.where(keep, pair, marks[odd]).astype(BF16)
            scores = lax.dot_general(
                head, keys[odd], (((1,), (1,)), ((), ())), preferred_element_type=F32
            )
            peak = jnp.max(scores, axis=1, keepdims=True)
            weights = jnp.exp2((scores - peak) * scale).astype(BF16)
            summed = jnp.dot(weights, values[odd], preferred_element_type=F32)
            part = summed[:, :128] / summed[:, 128:]
            if odd:
                parts[-1] = parts[-1] + part
            else:
                parts.append(part)
        attended = jnp.concatenate(parts, axis=1).astype(BF16)
        update = jnp.dot(attended, wo_ref[...], preferred_element_type=F32)
        done = (mixed.astype(F32) + update * live).astype(BF16)
        result[r] = done.reshape(SEGS, SIDE, C)

    def return_copy(r, s):
        return pltpu.make_async_remote_copy(
            src_ref=outgoing.at[r, s],
            dst_ref=out_ref.at[group % 16, pl.ds(SIDE * r, SIDE)],
            send_sem=send_out.at[r, s],
            recv_sem=recv_out.at[r, group % 16],
            device_id=(band, s),
            device_id_type=MESH,
        )

    def return_own(r):
        return pltpu.make_async_copy(
            outgoing.at[r, lon],
            out_ref.at[group % 16, pl.ds(SIDE * r, SIDE)],
            local_sem.at[1 + r],
        )

    def send_row(r):
        for s in range(SEGS):
            outgoing[r, s] = result[r, owner_ref[band, s]]

        @pl.when(mine)
        def _():
            return_own(r).start()

        def send(t, carry):
            s = (lon + 1 + t) % 16

            @pl.when(jnp.logical_or(band != lat, s != lon))
            def _():
                return_copy(r, s).start()

            return carry

        lax.fori_loop(0, 16, send, 0)

    for r in range(3):
        make_act(r)
    make_row(0)
    send_row(0)
    make_act(3)
    make_row(1)
    send_row(1)

    def drain(t, carry):
        @pl.when(16 * lat + t != group)
        def _():
            piece_copy(t).wait_send()

        @pl.when(group > 0)
        def _():
            halo_copy(t, True).wait_send()

        @pl.when(group < GROUPS - 1)
        def _():
            halo_copy(t, False).wait_send()

        @pl.when(jnp.logical_or(band != lat, t != lon))
        def _():
            for r in range(2):
                return_copy(r, t).wait_send()

        @pl.when(16 * lat + t != group)
        def _():
            for r in range(2):
                pltpu.make_async_remote_copy(
                    src_ref=outgoing.at[r, 0],
                    dst_ref=out_ref.at[t, pl.ds(SIDE * r, SIDE)],
                    send_sem=send_out.at[r, 0],
                    recv_sem=recv_out.at[r, t],
                    device_id=holder(16 * lat + t),
                    device_id_type=MESH,
                ).wait_recv()

        return carry

    lax.fori_loop(0, 16, drain, 0)

    @pl.when(mine)
    def _():
        for r in range(2):
            return_own(r).wait()


def turn_back(rotation_ref, block_ref, out_ref):
    quarter = rotation_ref[lax.axis_index("lat"), lax.axis_index("lon")]
    base, step_i, step_j = steps_of(quarter, False)

    def turn(at, carry):
        out_ref[pl.ds(at * 256, 256)] = turned(
            block_ref[...], base, step_i, step_j, at * 256, 256
        )
        return carry

    lax.fori_loop(0, 4, turn, 0)


def inverse_owner(owner):
    shards = jnp.arange(owner.shape[1], dtype=jnp.int32)
    matches = owner[:, None, :] == shards[None, :, None]
    return jnp.sum(jnp.where(matches, shards[None, None, :], 0), axis=2)


def on_device(
    fields, w_conv1, b_conv1, w_conv2, b_conv2, w_query, w_key, w_value, w_out,
    rotation, owner, counts,
):
    smem = pl.BlockSpec(memory_space=pltpu.SMEM)
    vmem = pl.BlockSpec(memory_space=pltpu.VMEM)
    hbm = pl.BlockSpec(memory_space=pl.ANY)
    dma = pltpu.SemaphoreType.DMA
    block = pl.pallas_call(
        section,
        name="section",
        out_shape=jax.ShapeDtypeStruct((SEGS, PIECE, C), BF16),
        in_specs=[smem] * 4 + [vmem, hbm, vmem, hbm, vmem] + [vmem] * 4,
        out_specs=vmem,
        scratch_shapes=[
            pltpu.VMEM((SEGS, PIECE, C), BF16),
            pltpu.VMEM((SEGS, PIECE, C), BF16),
            pltpu.VMEM((SEGS, PIECE, C), BF16),
            pltpu.VMEM((SEGS, PIECE, C), BF16),
            pltpu.VMEM((COLS, 6 * C), BF16),
            pltpu.VMEM((COLS, 4 * C), BF16),
            pltpu.VMEM((2, SEGS, SIDE, C), BF16),
            pltpu.VMEM((2, SEGS, SIDE, C), BF16),
            pltpu.VMEM((3 * C, 3 * C), BF16),
            pltpu.VMEM((3 * C, 3 * C), BF16),
            pltpu.VMEM((C, 8 * HEAD_DIM), BF16),
            dma((16,)),
            dma((16,)),
            dma((3, 16)),
            dma((3, 16)),
            dma((2, 16)),
            dma((2, 16)),
            dma((3,)),
            dma((2, 9)),
        ],
        compiler_params=pltpu.CompilerParams(
            collective_id=0, has_side_effects=True, vmem_limit_bytes=48 * 1024 * 1024
        ),
    )(
        rotation, inverse_owner(owner), owner, counts,
        fields.reshape(SIDE * SIDE, C), w_conv1, b_conv1.reshape(1, C), w_conv2,
        b_conv2.reshape(1, C), w_query, w_key, w_value, w_out,
    )
    turned_block = pl.pallas_call(
        turn_back,
        name="turn_back",
        out_shape=jax.ShapeDtypeStruct((SIDE * SIDE, C), BF16),
        in_specs=[smem, vmem],
        out_specs=vmem,
    )(rotation, block.reshape(SIDE * SIDE, C))
    return turned_block.reshape(SIDE, SIDE, C)


def solution(mesh):
    in_specs = (P("lat", "lon", None),) + (P(),) * 11
    out_specs = P("lat", "lon", None)
    return jax.shard_map(
        on_device, mesh=mesh, in_specs=in_specs, out_specs=out_specs, check_vma=False
    )
```

time: 504 us -> 70 us (0.14)
  blocking collectives: 315 us -> 0 us
  waiting for transfers between devices: 83.4 us -> 0 us
  Pallas kernels: 0 us -> 56.7 us
  between operations: 35.8 us -> 0.04 us
  local copies, waits for them, and re-layouts: 31.6 us -> 11.4 us
  other arithmetic: 16.2 us -> 1.04 us
  matrix products: 11.8 us -> 0 us
  starting transfers between devices: 8.66 us -> 0 us
    all_gather x8 -> x0, blocking collectives: 315 us -> none  [the longest x2 82.6 us: fetch_halo(): lax.all_gather(shortened(part[:, -width:]), 'lon', axis=0, tiled=True)]
    all_gather x1 -> x0, waiting for transfers between devices: 83.3 us -> none  [on_device(): piece = lax.all_gather(key_val, 'lon', axis=1, tiled=True)]
    pallas_call x0 -> x2, Pallas kernels: none -> 56.7 us  [the longest x1 53.4 us: on_device(): pl.pallas_call(section, name='section', out_shape=jax.ShapeDtypeStruct((S...]
    dot_general x23 -> x0, matrix products: 11.8 us -> none  [the longest x18 5.51 us: convolve(): jnp.dot(window, weight[i, j], preferred_element_type=jnp.float32)]
    slice x14 -> x0, local copies, waits for them, and re-layouts: 9.24 us -> none  [the longest x1 7.59 us: on_device(): piece[:, :, :head_dim]]
    ppermute x4 -> x0, starting transfers between devices: 8.65 us -> none  [passed_along(): return lax.ppermute(x, axis, pairs)]
    add x1 -> x0, other arithmetic: 5.62 us -> none  [on_device(): owner_row[positions // block_size] * block_size + positions % block_size]
    unnamed x28 -> x24, local copies, waits for them, and re-layouts: 13.4 us -> 11.4 us
  transfers between devices with their start and end apart: 5 -> 0, of which waited for: 1 -> 0; matrix products, arithmetic and copies ran while one was open for 3% -> 0% of each run, Pallas kernels for 0% -> 0%
where the time goes in v1:
time: 70 us; the launch traced here: 69.2 us
  Pallas kernels  56.7 us (81%)
  local copies, waits for them, and re-layouts  11.4 us (16%)
  other arithmetic  1.04 us (1%)
    pallas_call x1, Pallas kernels, on_device(): pl.pallas_call(section, name='section', out_shape=jax.ShapeDtypeStruct((S...  53.4 us
    unnamed x24, local copies, waits for them, and re-layouts  11.4 us
    pallas_call x1, Pallas kernels, on_device(): pl.pallas_call(turn_back, name='turn_back', out_shape=jax.ShapeDtypeStruc...  3.28 us

profile of v1, /device:TPU:2, one launch (start us, length us, event | category | flops | bytes accessed | tf_op | source)
XLA Modules:
  0.0 69.2 jit_solution(14340876940528016777)
XLA Ops:
  0.0 1.0 %select_reduce_fusion.inverse_ref = s32[16,16]{1,0:T(8,128)S(1)} fusion(s32[16,16]{1,0:T(8,128)} %owner_ref.1), kind=kLoop, calls=%fused_computation | loop fusion | flops 12032 | bytes 2048 | tf_op jit(solution)/shard_map/reduce_sum | solution.py:415
  1.0 0.9 %copy.15.wk_ref = bf16[256,64]{1,0:T(8,128)(2,1)S(1)} copy(bf16[256,64]{0,1:T(8,128)(2,1)} %param.18) | data formatting | bytes 65536 | tf_op args[6]
  1.9 0.9 %copy.16.wv_ref = bf16[256,64]{1,0:T(8,128)(2,1)S(1)} copy(bf16[256,64]{0,1:T(8,128)(2,1)} %param.19) | data formatting | bytes 65536 | tf_op args[7]
  2.8 0.0 copy-start.1
  2.8 1.3 %copy-done.1 = bf16[3,3,256,256]{3,2,1,0:T(8,128)(2,1)S(1)} copy-done((bf16[3,3,256,256]{3,2,1,0:T(8,128)(2,1)S(1)}, bf16[3,3,256,256]{3,2,1,0:T(8,128)(2,1)}, u32[]{:S(2)}) %copy-start.1) | copy-done | bytes 1179672
  4.1 0.0 copy-start.2
  4.1 1.3 %copy-done.2 = bf16[3,3,256,256]{3,2,1,0:T(8,128)(2,1)S(1)} copy-done((bf16[3,3,256,256]{3,2,1,0:T(8,128)(2,1)S(1)}, bf16[3,3,256,256]{3,2,1,0:T(8,128)(2,1)}, u32[]{:S(2)}) %copy-start.2) | copy-done | bytes 1179672
  5.4 0.0 copy-start.3
  5.4 1.0 %copy-done.3 = bf16[32,32,256]{2,1,0:T(8,128)(2,1)S(1)} copy-done((bf16[32,32,256]{2,1,0:T(8,128)(2,1)S(1)}, bf16[32,32,256]{2,1,0:T(8,128)(2,1)}, u32[]{:S(2)}) %copy-start.3) | copy-done | bytes 524312
  6.4 0.0 copy-start.4
  6.4 0.9 %copy-done.4 = bf16[256,256]{1,0:T(8,128)(2,1)S(1)} copy-done((bf16[256,256]{1,0:T(8,128)(2,1)S(1)}, bf16[256,256]{1,0:T(8,128)(2,1)}, u32[]{:S(2)}) %copy-start.4) | copy-done | bytes 131096
  7.3 0.9 %copy-done.5 = bf16[256,256]{1,0:T(8,128)(2,1)S(1)} copy-done((bf16[256,256]{1,0:T(8,128)(2,1)S(1)}, bf16[256,256]{1,0:T(8,128)(2,1)}, u32[]{:S(2)}) %copy-start.5) | copy-done | bytes 131096
  8.2 0.0 copy-start.6
  8.2 0.7 %copy-done.6 = s32[16,16]{1,0:T(8,128)S(1)} copy-done((s32[16,16]{1,0:T(8,128)S(1)}, s32[16,16]{1,0:T(8,128)}, u32[]{:S(2)}) %copy-start.6) | copy-done | bytes 1048
  8.9 0.0 copy-start.7
  8.9 0.7 %copy-done.7 = s32[16,16]{1,0:T(8,128)S(1)} copy-done((s32[16,16]{1,0:T(8,128)S(1)}, s32[16,16]{1,0:T(8,128)}, u32[]{:S(2)}) %copy-start.7) | copy-done | bytes 1048
  9.6 0.0 copy-start.8
  9.6 0.7 copy-done.8
  10.3 0.7 copy-done.9
  11.0 0.7 copy-done.10
  11.6 53.4 %section.1 = bf16[16,64,256]{2,1,0:T(8,128)(2,1)S(1)} custom-call(s32[16,16]{1,0:T(8,128)S(1)} %copy-done.6, s32[16,16]{1,0:T(8,128)S(1)} %select_reduce_fusion.inverse_ref, s32[16,16]{1,0:T(8,128)S(1)} %copy-done.7, s32[512]{0:T(512)S(1)} %copy-done.8, bf16[1024,256]{1,0:T(8,128)(2,1)S(1)} %bitcast.6, bf16[3,3,256,256]{3,2,1,0:T(8,128)(2,1)S(1)} %copy-done.1, ...), custom_call_target="tpu_custom_call" | custom-call | tf_op jit(solution)/shard_map/section/pallas_call | solution.py:426
  65.1 0.0 copy-start
  65.1 0.8 %copy-done = bf16[16,64,256]{2,1,0:T(8,128)(2,1)} copy-done((bf16[16,64,256]{2,1,0:T(8,128)(2,1)}, bf16[16,64,256]{2,1,0:T(8,128)(2,1)S(1)}, u32[]{:S(2)}) %copy-start) | copy-done | bytes 524312
  65.9 3.3 %turn_back.1 = bf16[1024,256]{1,0:T(8,128)(2,1)} custom-call(s32[16,16]{1,0:T(8,128)} %rotation_ref.3, bf16[1024,256]{1,0:T(8,128)(2,1)} %bitcast.5), custom_call_target="tpu_custom_call" | custom-call | tf_op jit(solution)/shard_map/turn_back/pallas_call | solution.py:461
  (3 shorter events, 0.0 us)
Async XLA Ops:
  2.8 1.3 %copy-start.1 = (bf16[3,3,256,256]{3,2,1,0:T(8,128)(2,1)S(1)}, bf16[3,3,256,256]{3,2,1,0:T(8,128)(2,1)}, u32[]{:S(2)}) copy-start(bf16[3,3,256,256]{3,2,1,0:T(8,128)(2,1)} %w1_hbm.1) | copy-start | bytes 3538948
  4.1 1.3 %copy-start.2 = (bf16[3,3,256,256]{3,2,1,0:T(8,128)(2,1)S(1)}, bf16[3,3,256,256]{3,2,1,0:T(8,128)(2,1)}, u32[]{:S(2)}) copy-start(bf16[3,3,256,256]{3,2,1,0:T(8,128)(2,1)} %w2_hbm.1) | copy-start | bytes 3538948
  5.4 1.0 %copy-start.3 = (bf16[32,32,256]{2,1,0:T(8,128)(2,1)S(1)}, bf16[32,32,256]{2,1,0:T(8,128)(2,1)}, u32[]{:S(2)}) copy-start(bf16[32,32,256]{2,1,0:T(8,128)(2,1)} %param.12) | copy-start | bytes 1572868
  6.4 0.9 %copy-start.4 = (bf16[256,256]{1,0:T(8,128)(2,1)S(1)}, bf16[256,256]{1,0:T(8,128)(2,1)}, u32[]{:S(2)}) copy-start(bf16[256,256]{1,0:T(8,128)(2,1)} %wq_ref.1) | copy-start | bytes 393220
  7.3 0.9 %copy-start.5 = (bf16[256,256]{1,0:T(8,128)(2,1)S(1)}, bf16[256,256]{1,0:T(8,128)(2,1)}, u32[]{:S(2)}) copy-start(bf16[256,256]{1,0:T(8,128)(2,1)} %wo_ref.1) | copy-start | bytes 393220
  8.2 0.7 %copy-start.6 = (s32[16,16]{1,0:T(8,128)S(1)}, s32[16,16]{1,0:T(8,128)}, u32[]{:S(2)}) copy-start(s32[16,16]{1,0:T(8,128)} %rotation_ref.3) | copy-start | bytes 3076
  8.9 0.7 %copy-start.7 = (s32[16,16]{1,0:T(8,128)S(1)}, s32[16,16]{1,0:T(8,128)}, u32[]{:S(2)}) copy-start(s32[16,16]{1,0:T(8,128)} %owner_ref.1) | copy-start | bytes 3076
  9.6 0.7 copy-start.8
  10.3 0.7 copy-start.9
  11.0 0.7 copy-start.10
  65.1 0.8 %copy-start = (bf16[16,64,256]{2,1,0:T(8,128)(2,1)}, bf16[16,64,256]{2,1,0:T(8,128)(2,1)S(1)}, u32[]{:S(2)}) copy-start(bf16[16,64,256]{2,1,0:T(8,128)(2,1)S(1)} %section.1) | copy-start | bytes 1572868

commit v2 on v1

--- a/solution.py
+++ b/solution.py
@@ -63,18 +63,35 @@
 
 
 def section(
-    rotation_ref, inverse_ref, owner_ref, counts_ref,
-    fields_ref, w1_hbm, b1_ref, w2_hbm, b2_ref,
-    wq_ref, wk_ref, wv_ref, wo_ref,
+    rotation_hbm, owner_hbm, counts_hbm,
+    fields_hbm, w1_hbm, b1_hbm, w2_hbm, b2_hbm,
+    wq_hbm, wk_hbm, wv_hbm, wo_hbm,
     out_ref,
+    rotation_ref, owner_ref, counts_ref, inverse_ref,
+    fields_ref, b1_ref, b2_ref, wq_ref, wk_ref, wv_ref, wo_ref,
     upright, raw_up, raw, raw_down, rows, acts, result, outgoing, w1, w2, wkv,
     send_in, recv_in, send_halo, recv_halo, send_out, recv_out, local_sem, weight_sem,
+    small_sem,
 ):
     lat, lon = lax.axis_index("lat"), lax.axis_index("lon")
     group = row_group(lat, lon)
     band = group // 16
     mine = band == lat
     barrier = pltpu.get_barrier_semaphore()
+
+    def small_copies():
+        pairs = (
+            (rotation_hbm, rotation_ref), (fields_hbm, fields_ref),
+            (owner_hbm, owner_ref), (counts_hbm, counts_ref),
+            (wk_hbm, wk_ref), (wv_hbm, wv_ref),
+            (b1_hbm, b1_ref), (b2_hbm, b2_ref), (wq_hbm, wq_ref), (wo_hbm, wo_ref),
+        )
+        for at, (source, target) in enumerate(pairs):
+            yield pltpu.make_async_copy(source, target, small_sem.at[at])
+
+    early = list(small_copies())
+    for copy in early[:2]:
+        copy.start()
 
     def greet(device):
         @pl.when(jnp.logical_or(device[0] != lat, device[1] != lon))
@@ -106,8 +123,12 @@
                         weight_sem.at[which, 3 * i + j],
                     )
 
+    for copy in early[2:]:
+        copy.start()
     for copy in weight_copies():
         copy.start()
+    for copy in early[:2]:
+        copy.wait()
 
     quarter = rotation_ref[lat, lon]
     base, step_i, step_j = steps_of(quarter, True)
@@ -127,12 +148,29 @@
     def _():
         raw_down[...] = jnp.zeros((SEGS, PIECE, C), BF16)
 
+    for copy in early[2:6]:
+        copy.wait()
     key_part = wk_ref[...]
     value_part = wv_ref[...]
-    blank = jnp.zeros((C, HEAD_DIM), BF16)
+    blank = jnp.zeros((HEAD_DIM, C), BF16)
     wkv[...] = jnp.concatenate(
-        [key_part, blank, blank, key_part, value_part, blank, blank, value_part], axis=1
-    )
+        [key_part, blank, blank, key_part, value_part, blank, blank, value_part], axis=0
+    ).T
+
+    def invert(t, carry):
+        for slot in range(3):
+            from_band = jnp.clip(group - 1 + slot, 0, GROUPS - 1) // 16
+            terms = [
+                jnp.where(owner_ref[from_band, s] == t, s, 0) for s in range(1, SEGS)
+            ]
+            while len(terms) > 1:
+                terms = [
+                    terms[k] + terms[k + 1] if k + 1 < len(terms) else terms[k]
+                    for k in range(0, len(terms), 2)
+                ]
+            inverse_ref[slot, t] = jnp.minimum(terms[0], SEGS - 1)
+        return carry
+
 
     own = jnp.where(mine, 1, 0)
     pl.semaphore_wait(
@@ -167,6 +205,7 @@
         return carry
 
     lax.fori_loop(0, 16, send_piece, 0)
+    lax.fori_loop(0, SEGS, invert, 0)
 
     def halo_copy(s, up):
         slot = 2 if up else 0
@@ -214,9 +253,8 @@
     lax.fori_loop(0, 16, forward, 0)
 
     def place(slot):
-        from_band = jnp.clip(group - 1 + slot, 0, GROUPS - 1) // 16
         for t in range(SEGS):
-            s = inverse_ref[from_band, t]
+            s = inverse_ref[slot, t]
             piece = (raw_up, raw, raw_down)[slot][s]
             for r in range(2):
                 rows[pl.ds(SIDE * t, SIDE), pl.ds(C * (2 * slot + r), C)] = piece[
@@ -224,6 +262,8 @@
                 ]
 
     place(1)
+    for copy in early[6:]:
+        copy.wait()
     for copy in weight_copies():
         copy.wait()
 
@@ -409,27 +449,32 @@
     lax.fori_loop(0, 4, turn, 0)
 
 
-def inverse_owner(owner):
-    shards = jnp.arange(owner.shape[1], dtype=jnp.int32)
-    matches = owner[:, None, :] == shards[None, :, None]
-    return jnp.sum(jnp.where(matches, shards[None, None, :], 0), axis=2)
-
-
 def on_device(
     fields, w_conv1, b_conv1, w_conv2, b_conv2, w_query, w_key, w_value, w_out,
     rotation, owner, counts,
 ):
     smem = pl.BlockSpec(memory_space=pltpu.SMEM)
     vmem = pl.BlockSpec(memory_space=pltpu.VMEM)
-    hbm = pl.BlockSpec(memory_space=pl.ANY)
+    hbm = pl.BlockSpec(memory_space=pltpu.HBM)
     dma = pltpu.SemaphoreType.DMA
     block = pl.pallas_call(
         section,
         name="section",
         out_shape=jax.ShapeDtypeStruct((SEGS, PIECE, C), BF16),
-        in_specs=[smem] * 4 + [vmem, hbm, vmem, hbm, vmem] + [vmem] * 4,
+        in_specs=[hbm] * 12,
         out_specs=vmem,
         scratch_shapes=[
+            pltpu.SMEM((16, 16), jnp.int32),
+            pltpu.SMEM((16, 16), jnp.int32),
+            pltpu.SMEM((2 * GROUPS,), jnp.int32),
+            pltpu.SMEM((3, SEGS), jnp.int32),
+            pltpu.VMEM((SIDE * SIDE, C), BF16),
+            pltpu.VMEM((1, C), F32),
+            pltpu.VMEM((1, C), F32),
+            pltpu.VMEM((C, C), BF16),
+            pltpu.VMEM((HEAD_DIM, C), BF16),
+            pltpu.VMEM((HEAD_DIM, C), BF16),
+            pltpu.VMEM((C, C), BF16),
             pltpu.VMEM((SEGS, PIECE, C), BF16),
             pltpu.VMEM((SEGS, PIECE, C), BF16),
             pltpu.VMEM((SEGS, PIECE, C), BF16),
@@ -449,14 +494,15 @@
             dma((2, 16)),
             dma((3,)),
             dma((2, 9)),
+            dma((10,)),
         ],
         compiler_params=pltpu.CompilerParams(
-            collective_id=0, has_side_effects=True, vmem_limit_bytes=48 * 1024 * 1024
+            collective_id=0, has_side_effects=True, vmem_limit_bytes=67043328
         ),
     )(
-        rotation, inverse_owner(owner), owner, counts,
+        rotation, owner, counts,
         fields.reshape(SIDE * SIDE, C), w_conv1, b_conv1.reshape(1, C), w_conv2,
-        b_conv2.reshape(1, C), w_query, w_key, w_value, w_out,
+        b_conv2.reshape(1, C), w_query, w_key.T, w_value.T, w_out,
     )
     turned_block = pl.pallas_call(
         turn_back,

time: 70 us -> 56.9 us (0.81)
  local copies, waits for them, and re-layouts: 11.4 us -> 0 us
  other arithmetic: 1.04 us -> 0 us
    unnamed x24 -> x0, local copies, waits for them, and re-layouts: 11.4 us -> none
    reduce_sum x1 -> x0, other arithmetic: 1.04 us -> none  [inverse_owner(): return jnp.sum(jnp.where(matches, shards[None, None, :], 0), axis=2)]
where the time goes in v2:
time: 56.9 us; the launch traced here: 56.7 us
  Pallas kernels  56.7 us (100%)
    pallas_call x1, Pallas kernels, on_device(): pl.pallas_call(section, name='section', out_shape=jax.ShapeDtypeStruct((S...  53.4 us
    pallas_call x1, Pallas kernels, on_device(): pl.pallas_call(turn_back, name='turn_back', out_shape=jax.ShapeDtypeStruc...  3.29 us

profile of v2, /device:TPU:2, one launch (start us, length us, event | category | flops | bytes accessed | tf_op | source)
XLA Modules:
  0.0 56.7 jit_solution(1619038275001219662)
XLA Ops:
  0.0 53.4 %section.1 = bf16[16,64,256]{2,1,0:T(8,128)(2,1)} custom-call(s32[16,16]{1,0:T(8,128)} %rotation_ref.1, s32[16,16]{1,0:T(8,128)} %owner_hbm.1, s32[512]{0:T(512)} %counts_hbm.1, bf16[1024,256]{1,0:T(8,128)(2,1)} %bitcast.8, bf16[3,3,256,256]{3,2,1,0:T(8,128)(2,1)} %w1_hbm.1, f32[1,256]{1,0:T(1,128)} %bitcast.11, bf16[3,3,256,256]{3,2,1,0:T(8,128)(2,1)} %w2_hbm.1, ...), custom_call_target="tpu_custom_call" | custom-call | tf_op jit(solution)/shard_map/section/pallas_call | solution.py:460
  53.4 3.3 %turn_back.1 = bf16[1024,256]{1,0:T(8,128)(2,1)} custom-call(s32[16,16]{1,0:T(8,128)} %rotation_ref.1, bf16[1024,256]{1,0:T(8,128)(2,1)} %bitcast.7), custom_call_target="tpu_custom_call" | custom-call | tf_op jit(solution)/shard_map/turn_back/pallas_call | solution.py:507

commit v3 on v2

--- a/solution.py
+++ b/solution.py
@@ -69,7 +69,7 @@
     out_ref,
     rotation_ref, owner_ref, counts_ref, inverse_ref,
     fields_ref, b1_ref, b2_ref, wq_ref, wk_ref, wv_ref, wo_ref,
-    upright, raw_up, raw, raw_down, rows, acts, result, outgoing, w1, w2, wkv,
+    upright, raw_up, raw, raw_down, rows, acts, mixed_rows, queries, outgoing, w1, w2, wkv,
     send_in, recv_in, send_halo, recv_halo, send_out, recv_out, local_sem, weight_sem,
     small_sem,
 ):
@@ -309,6 +309,9 @@
     scale = math.log2(math.e) / math.sqrt(HEAD_DIM)
     lanes = lax.broadcasted_iota(jnp.int32, (1, 2 * HEAD_DIM), 1)
     low = lanes < HEAD_DIM
+    marks = [
+        jnp.where(lanes == (0 if odd else HEAD_DIM), 1.0, 0.0) for odd in range(2)
+    ]
 
     def make_row(r):
         live = live_of(r)
@@ -319,38 +322,62 @@
         mean = jnp.mean(flat * flat, axis=1, keepdims=True)
         normed = (flat * lax.rsqrt(mean + 1e-06)).astype(BF16)
         query = jnp.dot(normed, wq_ref[...], preferred_element_type=F32)
+        mixed_rows[r] = mixed.reshape(SEGS, SIDE, C)
+        queries[r] = query.astype(BF16).reshape(SEGS, SIDE, C)
         key_val = jnp.dot(normed, wkv[...], preferred_element_type=F32)
         bias = jnp.where(live > 0, 0.0, -1e30)
         ones = jnp.broadcast_to(live, (COLS, 2 * HEAD_DIM)).astype(BF16)
-        keys, values, marks = [], [], []
+        keys, values = [], []
         for odd in range(2):
-            spot = jnp.where(lanes == (0 if odd else HEAD_DIM), 1.0, 0.0)
             pair = key_val[:, 128 * odd : 128 * (odd + 1)]
-            keys.append((pair + bias * spot).astype(BF16))
+            keys.append((pair + bias * marks[odd]).astype(BF16))
             pair = key_val[:, 256 + 128 * odd : 256 + 128 * (odd + 1)].astype(BF16)
             values.append(jnp.concatenate([pair, ones], axis=1))
-            marks.append(spot)
-        parts = []
-        for h in range(HEADS):
-            odd = h % 2
-            pair = query[:, 128 * (h // 2) : 128 * (h // 2 + 1)]
+        count = counts_ref[2 * group + r]
+        for offsets in ((3, 5), (4, 0), (2, 6), (1, 7)):
+            shards = [
+                2 * ((lon // 2 + offset) % 8) + high for offset in offsets for high in range(2)
+            ]
+            make_chunk(r, shards, count, keys, values)
+
+    cells = lax.broadcasted_iota(jnp.int32, (SIDE, 1), 0)
+
+    def make_chunk(r, shards, count, keys, values):
+        segs = [owner_ref[band, s] for s in shards]
+        query = jnp.concatenate([queries[r, t] for t in segs], axis=0)
+        mixed = jnp.concatenate([mixed_rows[r, t] for t in segs], axis=0)
+        live = jnp.concatenate(
+            [jnp.where(cells + SIDE * t < count, 1.0, 0.0) for t in segs], axis=0
+        )
+        size = 4 * SIDE
+        halves = []
+        for odd in range(2):
             keep = jnp.logical_not(low) if odd else low
-            head = jnp.where(keep, pair, marks[odd]).astype(BF16)
+            heads = jnp.concatenate([query[:, :128], query[:, 128:]], axis=0)
+            heads = jnp.where(keep, heads, marks[odd].astype(BF16))
             scores = lax.dot_general(
-                head, keys[odd], (((1,), (1,)), ((), ())), preferred_element_type=F32
+                heads, keys[odd], (((1,), (1,)), ((), ())), preferred_element_type=F32
             )
             peak = jnp.max(scores, axis=1, keepdims=True)
             weights = jnp.exp2((scores - peak) * scale).astype(BF16)
             summed = jnp.dot(weights, values[odd], preferred_element_type=F32)
-            part = summed[:, :128] / summed[:, 128:]
-            if odd:
-                parts[-1] = parts[-1] + part
-            else:
-                parts.append(part)
-        attended = jnp.concatenate(parts, axis=1).astype(BF16)
+            halves.append(summed[:, :128] / summed[:, 128:])
+        both = halves[0] + halves[1]
+        attended = jnp.concatenate([both[:size], both[size:]], axis=1).astype(BF16)
         update = jnp.dot(attended, wo_ref[...], preferred_element_type=F32)
-        done = (mixed.astype(F32) + update * live).astype(BF16)
-        result[r] = done.reshape(SEGS, SIDE, C)
+        done = (mixed.astype(F32) + update * live).astype(BF16).reshape(4, SIDE, C)
+        for k, s in enumerate(shards):
+            outgoing[r, s] = done[k]
+        for s in shards:
+            here = jnp.logical_and(mine, s == lon)
+
+            @pl.when(here)
+            def _():
+                return_own(r).start()
+
+            @pl.when(jnp.logical_not(here))
+            def _():
+                return_copy(r, s).start()
 
     def return_copy(r, s):
         return pltpu.make_async_remote_copy(
@@ -369,32 +396,11 @@
             local_sem.at[1 + r],
         )
 
-    def send_row(r):
-        for s in range(SEGS):
-            outgoing[r, s] = result[r, owner_ref[band, s]]
-
-        @pl.when(mine)
-        def _():
-            return_own(r).start()
-
-        def send(t, carry):
-            s = (lon + 1 + t) % 16
-
-            @pl.when(jnp.logical_or(band != lat, s != lon))
-            def _():
-                return_copy(r, s).start()
-
-            return carry
-
-        lax.fori_loop(0, 16, send, 0)
-
     for r in range(3):
         make_act(r)
     make_row(0)
-    send_row(0)
     make_act(3)
     make_row(1)
-    send_row(1)
 
     def drain(t, carry):
         @pl.when(16 * lat + t != group)
@@ -483,6 +489,7 @@
             pltpu.VMEM((COLS, 4 * C), BF16),
             pltpu.VMEM((2, SEGS, SIDE, C), BF16),
             pltpu.VMEM((2, SEGS, SIDE, C), BF16),
+            pltpu.VMEM((2, SEGS, SIDE, C), BF16),
             pltpu.VMEM((3 * C, 3 * C), BF16),
             pltpu.VMEM((3 * C, 3 * C), BF16),
             pltpu.VMEM((C, 8 * HEAD_DIM), BF16),

time: 56.9 us -> 55.9 us (0.982)
  Pallas kernels: 56.7 us -> 55.7 us
    pallas_call x1, Pallas kernels: 53.4 us -> 52.4 us  [on_device(): pl.pallas_call(section, name='section', out_shape=jax.ShapeDtypeStruct((S...]
where the time goes in v3:
time: 55.9 us; the launch traced here: 55.7 us
  Pallas kernels  55.7 us (100%)
    pallas_call x1, Pallas kernels, on_device(): pl.pallas_call(section, name='section', out_shape=jax.ShapeDtypeStruct((S...  52.4 us
    pallas_call x1, Pallas kernels, on_device(): pl.pallas_call(turn_back, name='turn_back', out_shape=jax.ShapeDtypeStruc...  3.29 us

profile of v3, /device:TPU:2, one launch (start us, length us, event | category | flops | bytes accessed | tf_op | source)
XLA Modules:
  0.0 55.7 jit_solution(9565728460233132849)
XLA Ops:
  0.0 52.4 %section.1 = bf16[16,64,256]{2,1,0:T(8,128)(2,1)} custom-call(s32[16,16]{1,0:T(8,128)} %rotation_ref.1, s32[16,16]{1,0:T(8,128)} %owner_hbm.1, s32[512]{0:T(512)} %counts_hbm.1, bf16[1024,256]{1,0:T(8,128)(2,1)} %bitcast.8, bf16[3,3,256,256]{3,2,1,0:T(8,128)(2,1)} %w1_hbm.1, f32[1,256]{1,0:T(1,128)} %bitcast.11, bf16[3,3,256,256]{3,2,1,0:T(8,128)(2,1)} %w2_hbm.1, ...), custom_call_target="tpu_custom_call" | custom-call | tf_op jit(solution)/shard_map/section/pallas_call | solution.py:466
  52.4 3.3 %turn_back.1 = bf16[1024,256]{1,0:T(8,128)(2,1)} custom-call(s32[16,16]{1,0:T(8,128)} %rotation_ref.1, bf16[1024,256]{1,0:T(8,128)(2,1)} %bitcast.7), custom_call_target="tpu_custom_call" | custom-call | tf_op jit(solution)/shard_map/turn_back/pallas_call | solution.py:514

commit v4 on v3

--- a/solution.py
+++ b/solution.py
@@ -71,7 +71,7 @@
     fields_ref, b1_ref, b2_ref, wq_ref, wk_ref, wv_ref, wo_ref,
     upright, raw_up, raw, raw_down, rows, acts, mixed_rows, queries, outgoing, w1, w2, wkv,
     send_in, recv_in, send_halo, recv_halo, send_out, recv_out, local_sem, weight_sem,
-    small_sem,
+    small_sem, partial,
 ):
     lat, lon = lax.axis_index("lat"), lax.axis_index("lon")
     group = row_group(lat, lon)
@@ -267,6 +267,21 @@
     for copy in weight_copies():
         copy.wait()
 
+    def mixed_taps(source, r, weight, low_tap, high_tap):
+        taps = jnp.dot(
+            source[:, C * (r + low_tap) : C * (r + high_tap)],
+            weight[C * low_tap : C * high_tap],
+            preferred_element_type=F32,
+        )
+        return (
+            pltpu.roll(taps[:, :C], 1, 0)
+            + taps[:, C : 2 * C]
+            + pltpu.roll(taps[:, 2 * C :], COLS - 1, 0)
+        )
+
+    for r, (low_tap, high_tap) in enumerate(((2, 3), (1, 3), (0, 2), (0, 1))):
+        partial[r] = mixed_taps(rows, r, w1, low_tap, high_tap) + b1_ref[...]
+
     def wait_halo(s, carry):
         @pl.when(group < GROUPS - 1)
         def _():
@@ -290,19 +305,9 @@
         count = jnp.where(inside, counts_ref[jnp.clip(row, 0, 2 * GROUPS - 1)], 0)
         return jnp.where(columns < count, 1.0, 0.0)
 
-    def convolved(source, r, weight, bias_ref):
-        taps = jnp.dot(
-            source[:, C * r : C * (r + 3)], weight[...], preferred_element_type=F32
-        )
-        return (
-            pltpu.roll(taps[:, :C], 1, 0)
-            + taps[:, C : 2 * C]
-            + pltpu.roll(taps[:, 2 * C :], COLS - 1, 0)
-            + bias_ref[...]
-        )
-
     def make_act(r):
-        first = convolved(rows, r, w1, b1_ref)
+        low_tap, high_tap = ((0, 2), (0, 1), (2, 3), (1, 3))[r]
+        first = mixed_taps(rows, r, w1, low_tap, high_tap) + partial[r]
         value = first / (1.0 + jnp.exp(-first))
         acts[:, C * r : C * (r + 1)] = (value * live_of(r - 1)).astype(BF16)
 
@@ -315,7 +320,7 @@
 
     def make_row(r):
         live = live_of(r)
-        second = convolved(acts, r, w2, b2_ref)
+        second = mixed_taps(acts, r, w2, 0, 3) + b2_ref[...]
         grid = rows[:, C * (r + 2) : C * (r + 3)].astype(F32)
         mixed = ((grid + second) * live).astype(BF16)
         flat = mixed.astype(F32)
@@ -502,6 +507,7 @@
             dma((3,)),
             dma((2, 9)),
             dma((10,)),
+            pltpu.VMEM((4, COLS, C), F32),
         ],
         compiler_params=pltpu.CompilerParams(
             collective_id=0, has_side_effects=True, vmem_limit_bytes=67043328

time: 55.9 us -> 55.1 us (0.986)
  Pallas kernels: 55.7 us -> 54.9 us
    pallas_call x1, Pallas kernels: 52.4 us -> 51.6 us  [on_device(): pl.pallas_call(section, name='section', out_shape=jax.ShapeDtypeStruct((S...]
where the time goes in v4:
time: 55.1 us; the launch traced here: 54.9 us
  Pallas kernels  54.9 us (100%)
    pallas_call x1, Pallas kernels, on_device(): pl.pallas_call(section, name='section', out_shape=jax.ShapeDtypeStruct((S...  51.6 us
    pallas_call x1, Pallas kernels, on_device(): pl.pallas_call(turn_back, name='turn_back', out_shape=jax.ShapeDtypeStruc...  3.29 us

profile of v4, /device:TPU:2, one launch (start us, length us, event | category | flops | bytes accessed | tf_op | source)
XLA Modules:
  0.0 54.9 jit_solution(3329621847672381836)
XLA Ops:
  0.0 51.6 %section.1 = bf16[16,64,256]{2,1,0:T(8,128)(2,1)} custom-call(s32[16,16]{1,0:T(8,128)} %rotation_ref.1, s32[16,16]{1,0:T(8,128)} %owner_hbm.1, s32[512]{0:T(512)} %counts_hbm.1, bf16[1024,256]{1,0:T(8,128)(2,1)} %bitcast.8, bf16[3,3,256,256]{3,2,1,0:T(8,128)(2,1)} %w1_hbm.1, f32[1,256]{1,0:T(1,128)} %bitcast.11, bf16[3,3,256,256]{3,2,1,0:T(8,128)(2,1)} %w2_hbm.1, ...), custom_call_target="tpu_custom_call" | custom-call | tf_op jit(solution)/shard_map/section/pallas_call | solution.py:471
  51.6 3.3 %turn_back.1 = bf16[1024,256]{1,0:T(8,128)(2,1)} custom-call(s32[16,16]{1,0:T(8,128)} %rotation_ref.1, bf16[1024,256]{1,0:T(8,128)(2,1)} %bitcast.7), custom_call_target="tpu_custom_call" | custom-call | tf_op jit(solution)/shard_map/turn_back/pallas_call | solution.py:520

commit v5 on v4

--- a/solution.py
+++ b/solution.py
@@ -138,24 +138,8 @@
         upright[pl.ds(4 * at, 4)] = part.reshape(4, PIECE, C)
         return carry
 
-    lax.fori_loop(0, 4, turn, 0)
-
-    @pl.when(group == 0)
-    def _():
-        raw_up[...] = jnp.zeros((SEGS, PIECE, C), BF16)
-
-    @pl.when(group == GROUPS - 1)
-    def _():
-        raw_down[...] = jnp.zeros((SEGS, PIECE, C), BF16)
-
-    for copy in early[2:6]:
-        copy.wait()
-    key_part = wk_ref[...]
-    value_part = wv_ref[...]
-    blank = jnp.zeros((HEAD_DIM, C), BF16)
-    wkv[...] = jnp.concatenate(
-        [key_part, blank, blank, key_part, value_part, blank, blank, value_part], axis=0
-    ).T
+    begin = group % 16 // 4
+    turn(begin, 0)
 
     def invert(t, carry):
         for slot in range(3):
@@ -191,20 +175,44 @@
     def own_copy():
         return pltpu.make_async_copy(upright.at[group % 16], raw.at[lon], local_sem.at[0])
 
+    def send_piece(j, carry):
+
+        @pl.when(16 * lat + j != group)
+        def _():
+            piece_copy(j).start()
+
+        return carry
+
+    lax.fori_loop(4 * begin, 4 * begin + 4, send_piece, 0)
+
     @pl.when(mine)
     def _():
         own_copy().start()
 
-    def send_piece(t, carry):
-        j = (group + 1 + t) % 16
-
-        @pl.when(16 * lat + j != group)
-        def _():
-            piece_copy(j).start()
-
-        return carry
-
-    lax.fori_loop(0, 16, send_piece, 0)
+    def turn_and_send(step, carry):
+        at = (begin + step) % 4
+        turn(at, 0)
+        return lax.fori_loop(4 * at, 4 * at + 4, send_piece, carry)
+
+    lax.fori_loop(1, 4, turn_and_send, 0)
+
+    @pl.when(group == 0)
+    def _():
+        raw_up[...] = jnp.zeros((SEGS, PIECE, C), BF16)
+
+    @pl.when(group == GROUPS - 1)
+    def _():
+        raw_down[...] = jnp.zeros((SEGS, PIECE, C), BF16)
+
+    for copy in early[2:6]:
+        copy.wait()
+    key_part = wk_ref[...]
+    value_part = wv_ref[...]
+    blank = jnp.zeros((HEAD_DIM, C), BF16)
+    wkv[...] = jnp.concatenate(
+        [key_part, blank, blank, key_part, value_part, blank, blank, value_part], axis=0
+    ).T
+
     lax.fori_loop(0, SEGS, invert, 0)
 
     def halo_copy(s, up):
@@ -451,13 +459,9 @@
     quarter = rotation_ref[lax.axis_index("lat"), lax.axis_index("lon")]
     base, step_i, step_j = steps_of(quarter, False)
 
-    def turn(at, carry):
-        out_ref[pl.ds(at * 256, 256)] = turned(
-            block_ref[...], base, step_i, step_j, at * 256, 256
-        )
-        return carry
-
-    lax.fori_loop(0, 4, turn, 0)
+    out_ref[...] = turned(
+        block_ref[...], base, step_i, step_j, pl.program_id(0) * 256, 256
+    )
 
 
 def on_device(
@@ -521,8 +525,9 @@
         turn_back,
         name="turn_back",
         out_shape=jax.ShapeDtypeStruct((SIDE * SIDE, C), BF16),
-        in_specs=[smem, vmem],
-        out_specs=vmem,
+        grid=(4,),
+        in_specs=[smem, pl.BlockSpec((SIDE * SIDE, C), lambda at: (0, 0))],
+        out_specs=pl.BlockSpec((256, C), lambda at: (at, 0)),
     )(rotation, block.reshape(SIDE * SIDE, C))
     return turned_block.reshape(SIDE, SIDE, C)
 

time: 55.1 us -> 55.5 us (level)
  no operation moved by 1% of the time
where the time goes in v5:
time: 55.5 us; the launch traced here: 55 us
  Pallas kernels  55 us (99%)
    pallas_call x1, Pallas kernels, on_device(): pl.pallas_call(section, name='section', out_shape=jax.ShapeDtypeStruct((S...  51.5 us
    pallas_call x1, Pallas kernels, on_device(): pl.pallas_call(turn_back, name='turn_back', out_shape=jax.ShapeDtypeStruc...  3.5 us

profile of v5, /device:TPU:2, one launch (start us, length us, event | category | flops | bytes accessed | tf_op | source)
XLA Modules:
  0.0 55.0 jit_solution(13657761599378492013)
XLA Ops:
  0.0 51.5 %section.1 = bf16[16,64,256]{2,1,0:T(8,128)(2,1)} custom-call(s32[16,16]{1,0:T(8,128)} %rotation_ref.1, s32[16,16]{1,0:T(8,128)} %owner_hbm.1, s32[512]{0:T(512)} %counts_hbm.1, bf16[1024,256]{1,0:T(8,128)(2,1)} %bitcast.8, bf16[3,3,256,256]{3,2,1,0:T(8,128)(2,1)} %w1_hbm.1, f32[1,256]{1,0:T(1,128)} %bitcast.11, bf16[3,3,256,256]{3,2,1,0:T(8,128)(2,1)} %w2_hbm.1, ...), custom_call_target="tpu_custom_call" | custom-call | tf_op jit(solution)/shard_map/section/pallas_call | solution.py:475
  51.5 3.5 %turn_back.1 = bf16[1024,256]{1,0:T(8,128)(2,1)} custom-call(s32[16,16]{1,0:T(8,128)} %rotation_ref.1, bf16[1024,256]{1,0:T(8,128)(2,1)} %bitcast.7), custom_call_target="tpu_custom_call" | custom-call | tf_op jit(solution)/shard_map/turn_back/pallas_call | solution.py:524
